TPU v7x, 32 devices: a whole 2x2x4 slice. The times are simulated.
32 devices in a mesh: rep: 8 (over z, y), zero: 4 (over x, core).
Axes of the slice: x: 2, y: 2, z: 4, core: 2. Of those that a mesh axis runs over, the one named last changes fastest.
Arguments:
- tokens: bfloat16 [12288, 1280], P(('rep', 'zero')), may hold values from -6 to 6
- cotangent: bfloat16 [12288, 1280], P(('rep', 'zero')), may hold values from -6 to 6
- weights: bfloat16 [1280, 6, 1280], P('zero')
- vectors: bfloat16 [5, 1280], P(None, 'zero')
- error: float32 [10240, 6, 1280], P(('rep', 'zero'))
- previous_right_factors: float32 [6, 1280, 32], P(None, None, 'zero'), may hold values from -6 to 6
- momentum: float32 [1280, 6, 1280], P('zero', None, 'rep')
- vec_momentum: float32 [5, 1280], P(None, 'zero')
- prompt_len: int32 [8], P('rep'), may hold values from 512 to 1024, as said below
Outputs:
- result: bfloat16 [12288, 1280], P(('rep', 'zero'))
- grad_tokens: float32 [12288, 1280], P(('rep', 'zero'))
- grad_weights: float32 [1280, 6, 1280], P('zero', None, 'rep')
- grad_vectors: float32 [5, 1280], P(None, 'zero')
- new_error: float32 [10240, 6, 1280], P(('rep', 'zero'))
- fresh_right_factors: float32 [6, 1280, 32], P(None, None, 'zero')
- new_momentum: float32 [1280, 6, 1280], P('zero', None, 'rep')
- new_vec_momentum: float32 [5, 1280], P(None, 'zero')
- update_weights: float32 [1280, 6, 1280], P('zero', None, 'rep')
- update_vectors: float32 [5, 1280], P(None, 'zero')
Inputs may be any that keep to these rules, and one draw needn't show every extreme that they name: `prompt_len`: valid prompt rows of a group; the other prompt rows of its 1024 are padding.
All inputs are finite; a program needn't handle non-finite values.
Results may differ from a plain program's by a relative error of at most 0.028.
Values may be sent and summed in bfloat16 or wider, within the bound.
No kernel may reach another device: no remote copies, remote signals or barrier semaphores. Data moves between devices by JAX's collectives and lax.ppermute only.
A program may use at most 320 MiB of HBM per device.

v0:
```python
import math

import jax
import jax.numpy as jnp
from jax import lax
from jax.sharding import PartitionSpec as P

HEADS = 16
PROMPT = 1024


EPS = 1e-06
MU = 0.9
LOG2E = 1.442695041
NEG = -1e30
PRECISION_HIGH = lax.Precision.HIGHEST


def rms_scale(field):
    return lax.rsqrt(jnp.mean(field * field, axis=-1, keepdims=True) + EPS)


def norm_back(field, scale, gain_vec, grad_in):
    weighted = grad_in * gain_vec
    inner = jnp.mean(field * weighted, axis=-1, keepdims=True)
    return scale * weighted - field * (scale * scale * scale) * inner


def orthonormal(factor):
    columns = []
    for col_index in range(factor.shape[-1]):
        column = factor[..., col_index]
        for earlier in columns:
            column = column - jnp.sum(earlier * column, axis=-2, keepdims=True) * earlier
        column = column * lax.rsqrt(jnp.sum(column * column, axis=-2, keepdims=True) + EPS)
        columns.append(column)
    return jnp.stack(columns, axis=-1)


def on_device(
    tokens,
    cotangent,
    weights,
    vectors,
    error,
    previous_right_factors,
    momentum,
    vec_momentum,
    prompt_len,
):
    f32 = jnp.float32
    bf16 = jnp.bfloat16
    zero_index = lax.axis_index("zero")
    rep_index = lax.axis_index("rep")
    zero_count = lax.axis_size("zero")
    rep_count = lax.axis_size("rep")
    tok_rows, feat_width = tokens.shape
    head_dim = feat_width // HEADS
    prompt_rows = PROMPT // zero_count
    prompt_valid = prompt_len[0]
    full_w, full_v = (
        lax.all_gather(weights, "zero", axis=0, tiled=True),
        lax.all_gather(vectors, "zero", axis=1, tiled=True),
    )
    vec_float = full_v.astype(f32)
    gain_one = vec_float[0]
    gain_two = vec_float[1]
    bias_one = vec_float[2]
    bias_two = vec_float[3]
    scale_raw = vec_float[4]
    tok_float = tokens.astype(f32)
    scale_one = rms_scale(tok_float)
    normed_one = (tok_float * scale_one * gain_one).astype(bf16)
    projected = jnp.einsum("ti,omi->mto", normed_one, full_w[:, 0:3, :], preferred_element_type=f32)
    query = projected[0]
    key_low = projected[1].astype(bf16)
    value_low = projected[2].astype(bf16)
    scale_const = LOG2E / math.sqrt(head_dim)
    query_scale = scale_const * jax.nn.softplus(scale_raw)
    scaled = (query * query_scale).astype(bf16)
    key_far, value_far = (
        lax.all_gather(key_low[:prompt_rows], "zero", axis=0, tiled=True),
        lax.all_gather(value_low[:prompt_rows], "zero", axis=0, tiled=True),
    )
    key_rows = jnp.concatenate([key_far, key_low[prompt_rows:]], axis=0)
    value_rows = jnp.concatenate([value_far, value_low[prompt_rows:]], axis=0)
    key_count = key_rows.shape[0]
    q_row = lax.broadcasted_iota(jnp.int32, (tok_rows, key_count), 0)
    k_col = lax.broadcasted_iota(jnp.int32, (tok_rows, key_count), 1)
    q_prompt = q_row < prompt_rows
    q_pos = zero_index * prompt_rows + q_row
    k_prompt = k_col < PROMPT
    see_prompt = k_prompt & (k_col < prompt_valid) & (jnp.logical_not(q_prompt) | (k_col <= q_pos))
    see_cont = (
        jnp.logical_not(k_prompt)
        & jnp.logical_not(q_prompt)
        & (k_col - PROMPT <= q_row - prompt_rows)
    )
    allowed = see_prompt | see_cont
    q_heads = scaled.reshape(tok_rows, HEADS, head_dim)
    k_heads = key_rows.reshape(key_count, HEADS, head_dim)
    v_heads = value_rows.reshape(key_count, HEADS, head_dim)

    def masked_scores():
        raw_scores = jnp.einsum("thd,khd->htk", q_heads, k_heads, preferred_element_type=f32)
        return jnp.where(allowed[None], raw_scores, NEG)

    masked = masked_scores()
    row_top = jnp.max(masked, axis=-1, keepdims=True)
    log_total = row_top + jnp.log(jnp.sum(jnp.exp(masked - row_top), axis=-1, keepdims=True))
    probs = jnp.exp(masked - log_total)
    attended = (
        jnp.einsum("htk,khd->thd", probs.astype(bf16), v_heads, preferred_element_type=f32)
        .reshape(tok_rows, feat_width)
        .astype(bf16)
    )
    branch = jnp.einsum("ti,oi->to", attended, full_w[:, 3, :], preferred_element_type=f32)
    hidden = tok_float + branch
    scale_two = rms_scale(hidden)
    normed_two = (hidden * scale_two * gain_two).astype(bf16)
    upper = (
        jnp.einsum("ti,oi->to", normed_two, full_w[:, 4, :], preferred_element_type=f32) + bias_one
    )
    activ = jax.nn.silu(upper).astype(bf16)
    output = jnp.einsum("ti,oi->to", activ, full_w[:, 5, :], preferred_element_type=f32) + bias_two
    result = (hidden + output).astype(bf16)
    back_w = lax.all_gather(weights, "zero", axis=0, tiled=True)
    grad_out = cotangent.astype(f32)
    grad_f = grad_out.astype(bf16)
    grad_act = jnp.einsum("to,oi->ti", grad_f, back_w[:, 5, :], preferred_element_type=f32)
    gate_sig = jax.nn.sigmoid(upper)
    grad_up = (grad_act * gate_sig * (1.0 + upper * (1.0 - gate_sig))).astype(bf16)
    grad_n2 = jnp.einsum("to,oi->ti", grad_up, back_w[:, 4, :], preferred_element_type=f32)
    grad_gain_two = jnp.sum(grad_n2 * hidden * scale_two, axis=0)
    grad_hidden = grad_out + norm_back(hidden, scale_two, gain_two, grad_n2)
    grad_branch = grad_hidden.astype(bf16)
    grad_att = jnp.einsum(
        "to,oi->ti", grad_branch, back_w[:, 3, :], preferred_element_type=f32
    ).astype(bf16)
    grad_att_heads = grad_att.reshape(tok_rows, HEADS, head_dim)
    probs_again = jnp.exp(masked_scores() - log_total)
    grad_probs = jnp.einsum("thd,khd->htk", grad_att_heads, v_heads, preferred_element_type=f32)
    delta = jnp.sum(probs_again * grad_probs, axis=-1, keepdims=True)
    grad_scores = (probs_again * (grad_probs - delta)).astype(bf16)
    grad_values = jnp.einsum(
        "htk,thd->khd", probs_again.astype(bf16), grad_att_heads, preferred_element_type=f32
    ).reshape(key_count, feat_width)
    grad_keys = jnp.einsum(
        "htk,thd->khd", grad_scores, q_heads, preferred_element_type=f32
    ).reshape(key_count, feat_width)
    grad_sq = jnp.einsum("htk,khd->thd", grad_scores, k_heads, preferred_element_type=f32).reshape(
        tok_rows, feat_width
    )
    own_keys, own_values = (
        lax.psum_scatter(
            grad_keys[:PROMPT].astype(jnp.bfloat16), "zero", scatter_dimension=0, tiled=True
        ).astype(jnp.float32),
        lax.psum_scatter(
            grad_values[:PROMPT].astype(jnp.bfloat16), "zero", scatter_dimension=0, tiled=True
        ).astype(jnp.float32),
    )
    grad_key = jnp.concatenate([own_keys, grad_keys[PROMPT:]], axis=0).astype(bf16)
    grad_value = jnp.concatenate([own_values, grad_values[PROMPT:]], axis=0).astype(bf16)
    grad_query = (grad_sq * query_scale).astype(bf16)
    grad_scale_raw = jnp.sum(grad_sq * query, axis=0) * scale_const * jax.nn.sigmoid(scale_raw)
    grad_proj = jnp.stack([grad_query, grad_key, grad_value], axis=0)
    grad_n1 = jnp.einsum("mto,omi->ti", grad_proj, back_w[:, 0:3, :], preferred_element_type=f32)
    grad_gain_one = jnp.sum(grad_n1 * tok_float * scale_one, axis=0)
    grad_tokens = grad_hidden + norm_back(tok_float, scale_one, gain_one, grad_n1)
    grad_stack = jnp.stack([grad_query, grad_key, grad_value, grad_branch, grad_up, grad_f], axis=0)
    input_stack = jnp.stack(
        [normed_one, normed_one, normed_one, attended, normed_two, activ], axis=0
    )
    grad_block = lax.psum_scatter(
        jnp.einsum("mto,mti->omi", grad_stack, input_stack, preferred_element_type=f32).astype(
            jnp.bfloat16
        ),
        "zero",
        scatter_dimension=0,
        tiled=True,
    ).astype(jnp.float32)
    vec_terms = jnp.stack(
        [
            grad_gain_one,
            grad_gain_two,
            jnp.sum(grad_up.astype(f32), axis=0),
            jnp.sum(grad_f.astype(f32), axis=0),
            grad_scale_raw,
        ],
        axis=0,
    )
    vec_block = lax.psum_scatter(vec_terms, "zero", scatter_dimension=1, tiled=True)
    combined_result = grad_block + error
    local_left_factor = jnp.einsum(
        "edn,dnw->edw", combined_result, previous_right_factors, precision=PRECISION_HIGH
    )
    vec_total = lax.psum(vec_block, "rep")
    left_parts = []
    right_parts = []
    for mat_index in range(combined_result.shape[1]):
        left_sum = lax.psum(local_left_factor[:, mat_index], "rep")
        left_ortho = orthonormal(left_sum[:, None, :] / rep_count)[:, 0, :]
        right_term = jnp.einsum(
            "oi,or->ir", combined_result[:, mat_index], left_ortho, precision=PRECISION_HIGH
        )
        right_parts.append(lax.psum(right_term.astype(jnp.bfloat16), "rep").astype(jnp.float32))
        left_parts.append(left_ortho)
    orthogonalized = jnp.stack(left_parts, axis=1)
    right_total = jnp.stack(right_parts, axis=0)
    fresh_right_factors = right_total / rep_count
    approximation = jnp.einsum(
        "upt,pqt->upq", orthogonalized, fresh_right_factors, precision=PRECISION_HIGH
    )
    new_error = combined_result - approximation
    rep_width = feat_width // rep_count
    grad_weights = lax.dynamic_slice_in_dim(approximation, rep_index * rep_width, rep_width, 2)
    step_rate = 0.03 / math.sqrt(zero_count * tok_rows)
    new_momentum = MU * momentum + grad_weights
    update_weights = -step_rate * new_momentum
    grad_vectors = vec_total / rep_count
    new_vec_momentum = MU * vec_momentum + grad_vectors
    update_vectors = -step_rate * new_vec_momentum
    return (
        result,
        grad_tokens,
        grad_weights,
        grad_vectors,
        new_error,
        fresh_right_factors,
        new_momentum,
        new_vec_momentum,
        update_weights,
        update_vectors,
    )


def solution(mesh):
    in_specs = (
        P(("rep", "zero"), None),
        P(("rep", "zero"), None),
        P("zero", None, None),
        P(None, "zero"),
        P(("rep", "zero"), None, None),
        P(None, None, "zero"),
        P("zero", None, "rep"),
        P(None, "zero"),
        P("rep"),
    )
    out_specs = (
        P(("rep", "zero"), None),
        P(("rep", "zero"), None),
        P("zero", None, "rep"),
        P(None, "zero"),
        P(("rep", "zero"), None, None),
        P(None, None, "zero"),
        P("zero", None, "rep"),
        P(None, "zero"),
        P("zero", None, "rep"),
        P(None, "zero"),
    )
    return jax.shard_map(
        on_device, mesh=mesh, in_specs=in_specs, out_specs=out_specs, check_vma=False
    )
```

profile of v0, /device:TPU:0, one launch (start us, length us, event | category | flops | bytes accessed | tf_op | source)
XLA Modules:
  0.0 1215.3 jit_solution(3644075702543074997)
XLA Ops:
  8.0 6.2 all-gather.2
  15.9 120.7 %all-gather.7.cloned.1.call-done = bf16[1280,6,1280]{2,0,1:T(8,128)(2,1)} async-done(((bf16[320,6,1280]{2,0,1:T(8,128)(2,1)}), bf16[1280,6,1280]{2,0,1:T(8,128)(2,1)}) %all-gather.7.cloned.1.call-update) | async-done | bytes 19660816 | tf_op jit(solution)/shard_map/all_gather | solution.py:62
  136.6 10.4 fusion.115
  163.3 12.1 all-gather.9.cloned.1.call-done
  175.4 27.7 %all-gather.11.cloned.1.call-done = bf16[1,1024,1280]{2,1,0:T(8,128)(2,1)} async-done(((bf16[1,256,1280]{2,1,0:T(8,128)(2,1)}), bf16[1,1024,1280]{2,1,0:T(8,128)(2,1)}) %all-gather.11.cloned.1.call-update) | async-done | bytes 2621456 | tf_op jit(solution)/shard_map/all_gather | solution.py:82
  218.6 13.1 %select_reduce_fusion = (f32[16,384]{1,0:T(8,128)S(1)}, f32[16,384,1152]{2,1,0:T(8,128)}) fusion(pred[384,1152]{1,0:T(8,128)(4,1)} %fusion.50, bf16[1152,16,80]{0,2,1:T(8,128)(2,1)} %bitcast.662, f32[384,16,80]{0,2,1:T(8,128)S(1)} %bitcast.659, f32[16,80]{1,0:T(8,128)S(1)} %mul.16566), kind=kOutput, calls=%fused_computation.5 | convolution fusion | flops 1147594752 | bytes 33698816 | tf_op jit(solution)/shard_map/thd,khd->htk/dot_general | solution.py:105
  231.6 13.7 %exponential_reduce_fusion = f32[16,384]{1,0:T(8,128)S(1)} fusion(f32[16,384,1152]{2,1,0:T(8,128)} %get-tuple-element.459, f32[16,384]{1,0:T(8,128)S(1)} %get-tuple-element.458, pred[384,1152]{1,0:T(8,128)(4,1)S(1)} %copy-done.3), kind=kLoop, calls=%fused_computation.3 | loop fusion | flops 21227520 | bytes 28803072 | tf_op jit(solution)/shard_map/reduce_sum | solution.py:110
  245.3 13.1 %fusion.51 = bf16[16,80,384]{2,1,0:T(8,128)(2,1)} fusion(bf16[1152,16,80]{0,2,1:T(8,128)(2,1)S(1)} %bitcast.665, f32[16,384,1152]{2,1,0:T(8,128)} %get-tuple-element.459, f32[16,384]{1,0:T(8,128)S(1)} %log_add_fusion, pred[384,1152]{1,0:T(8,128)(4,1)S(1)} %copy-done.3), kind=kOutput, calls=%fused_computation.96 | convolution fusion | flops 1154187264 | bytes 32710656 | tf_op jit(solution)/shard_map/htk,khd->thd/dot_general | solution.py:113
  289.8 24.5 %multiply_reduce_fusion = (f32[16,384]{1,0:T(8,128)S(1)}, f32[16,384,1152]{2,1,0:T(8,128)}) fusion(f32[16,384,1152]{2,1,0:T(8,128)} %get-tuple-element.459, f32[16,384]{1,0:T(8,128)S(1)} %log_add_fusion, pred[384,1152]{1,0:T(8,128)(4,1)} %fusion.50, bf16[384,16,80]{0,2,1:T(8,128)(2,1)} %bitcast.669, bf16[1152,16,80]{0,2,1:T(8,128)(2,1)} %bitcast.664), kind=kOutput, calls=%fused_computation.1 | convolution fusion | flops 1160767488 | bytes 61046784 | tf_op jit(solution)/shard_map/thd,khd->htk/dot_general | solution.py:142
  314.3 23.7 %multiply_convert_fusion = bf16[16,384,1152]{2,1,0:T(8,128)(2,1)} fusion(f32[16,384,1152]{2,1,0:T(8,128)} %get-tuple-element.464, f32[16,384,1152]{2,1,0:T(8,128)} %get-tuple-element.459, f32[16,384]{1,0:T(8,128)S(1)} %get-tuple-element.463, f32[16,384]{1,0:T(8,128)S(1)} %log_add_fusion, pred[384,1152]{1,0:T(8,128)(4,1)} %fusion.50), kind=kLoop, calls=%fused_computation | loop fusion | flops 35389440 | bytes 71270400 | tf_op jit(solution)/shard_map/convert_element_type | solution.py:144
  338.1 8.0 fusion.8
  354.1 14.2 %fusion.9 = bf16[1152,16,80]{0,2,1:T(8,128)(2,1)S(1)} fusion(bf16[384,16,80]{0,2,1:T(8,128)(2,1)} %bitcast.670, f32[16,384,1152]{2,1,0:T(8,128)} %get-tuple-element.459, f32[16,384]{1,0:T(8,128)S(1)} %log_add_fusion, pred[384,1152]{1,0:T(8,128)(4,1)} %fusion.50), kind=kOutput, calls=%fused_computation.23 | convolution fusion | flops 1155170304 | bytes 32710656 | tf_op jit(solution)/shard_map/htk,thd->khd/dot_general | solution.py:145
  380.8 11.7 fusion.44
  401.2 24.4 %reduce-scatter.11.cloned.1.call-done = bf16[256,1280]{1,0:T(8,128)(2,1)} async-done(((bf16[1024,1280]{1,0:T(8,128)(2,1)}), bf16[256,1280]{1,0:T(8,128)(2,1)}) %reduce-scatter.11.cloned.1.call-update) | async-done | bytes 655376 | tf_op jit(solution)/shard_map/reduce_scatter | solution.py:158
  431.0 9.2 fusion.43
  442.1 17.9 %convolution_convert_fusion = bf16[6,1280,1280]{2,1,0:T(8,128)(2,1)} fusion(bf16[6,384,1280]{2,1,0:T(8,128)(2,1)} %get-tuple-element.466, bf16[6,384,1280]{2,1,0:T(8,128)(2,1)} %bitcast_dynamic-update-slice_fusion), kind=kOutput, calls=%fused_computation.4 | convolution fusion | flops 7559577600 | bytes 31457280 | tf_op jit(solution)/shard_map/mto,mti->omi/dot_general | solution.py:175
  460.0 26.4 %copy.101 = bf16[1280,7680]{1,0:T(8,128)(2,1)} copy(bf16[1280,7680]{0,1:T(8,128)(2,1)} %bitcast.668) | data formatting | bytes 39321600
  489.6 6.5 fusion.27
  497.8 131.3 %reduce-scatter.13.cloned.1.call-done = bf16[320,7680]{1,0:T(8,128)(2,1)} async-done(((bf16[1280,7680]{1,0:T(8,128)(2,1)}), bf16[320,7680]{1,0:T(8,128)(2,1)}) %reduce-scatter.13.cloned.1.call-update) | async-done | bytes 4915216
  629.1 8.0 copy.102
  637.1 8.6 copy.91
  645.7 10.3 convert_add_fusion
  656.0 10.7 convolution_bitcast_fusion
  671.0 68.0 %all-reduce.5.cloned.1.call-done = (f32[320,8]{0,1:T(8,128)}, f32[320,8]{0,1:T(8,128)}, f32[320,8]{0,1:T(8,128)}, f32[320,8]{0,1:T(8,128)}, f32[320,8]{0,1:T(8,128)}, /*index=5*/f32[320,8]{0,1:T(8,128)}, f32[5,320]{1,0:T(8,128)}) async-done(((f32[320,8]{0,1:T(8,128)}, f32[320,8]{0,1:T(8,128)}, f32[320,8]{0,1:T(8,128)}, f32[320,8]{0,1:T(8,128)}, f32[320,8]{0,1:T(8,128)}, /*index=5*/f32[320,8]{0,1:T(8,128)}, ...) | async-done | bytes 67856 | tf_op jit(solution)/shard_map/psum | solution.py:201
  780.5 17.7 %subtract_multiply_fusion.35 = (f32[320,1,1]{0,2,1:T(1,128)S(1)}, f32[320,1,1]{0,2,1:T(1,128)S(1)}, f32[320,1,1]{0,2,1:T(1,128)S(1)}, f32[320,1,1]{0,2,1:T(1,128...) fusion(f32[320,1,1]{0,2,1:T(1,128)S(1)} %get-tuple-element.437, ...), kind=kLoop, calls=%fused_computation.622 | loop fusion | flops 20160 | bytes 19340 | tf_op jit(solution)/shard_map/mul | solution.py:35
  842.7 17.6 %subtract_multiply_fusion.28 = (f32[320,1,1]{0,2,1:T(1,128)S(1)}, f32[320,1,1]{0,2,1:T(1,128)S(1)}, f32[320,1,1]{0,2,1:T(1,128)S(1)}, f32[320,1,1]{0,2,1:T(1,128...) fusion(f32[320,1,1]{0,2,1:T(1,128)S(1)} %get-tuple-element.404, ...), kind=kLoop, calls=%fused_computation.566 | loop fusion | flops 20160 | bytes 19340 | tf_op jit(solution)/shard_map/mul | solution.py:35
  904.0 17.6 %subtract_multiply_fusion.21 = (f32[320,1,1]{0,2,1:T(1,128)S(1)}, f32[320,1,1]{0,2,1:T(1,128)S(1)}, f32[320,1,1]{0,2,1:T(1,128)S(1)}, f32[320,1,1]{0,2,1:T(1,128...) fusion(f32[320,1,1]{0,2,1:T(1,128)S(1)} %get-tuple-element.371, ...), kind=kLoop, calls=%fused_computation.510 | loop fusion | flops 20160 | bytes 19340 | tf_op jit(solution)/shard_map/mul | solution.py:35
  965.4 17.6 %subtract_multiply_fusion.14 = (f32[320,1,1]{0,2,1:T(1,128)S(1)}, f32[320,1,1]{0,2,1:T(1,128)S(1)}, f32[320,1,1]{0,2,1:T(1,128)S(1)}, f32[320,1,1]{0,2,1:T(1,128...) fusion(f32[320,1,1]{0,2,1:T(1,128)S(1)} %get-tuple-element.338, ...), kind=kLoop, calls=%fused_computation.454 | loop fusion | flops 20160 | bytes 19340 | tf_op jit(solution)/shard_map/mul | solution.py:35
  1026.8 17.6 %subtract_multiply_fusion.7 = (f32[320,1,1]{0,2,1:T(1,128)S(1)}, f32[320,1,1]{0,2,1:T(1,128)S(1)}, f32[320,1,1]{0,2,1:T(1,128)S(1)}, f32[320,1,1]{0,2,1:T(1,128)...) fusion(f32[320,1,1]{0,2,1:T(1,128)S(1)} %get-tuple-element.305, ...), kind=kLoop, calls=%fused_computation.398 | loop fusion | flops 20160 | bytes 19340 | tf_op jit(solution)/shard_map/mul | solution.py:35
  1088.3 17.5 %subtract_multiply_fusion = (f32[320,1,1]{0,2,1:T(1,128)S(1)}, f32[320,1,1]{0,2,1:T(1,128)S(1)}, f32[320,1,1]{0,2,1:T(1,128)S(1)}, f32[320,1,1]{0,2,1:T(1,128)S(...) fusion(f32[320,1,1]{0,2,1:T(1,128)S(1)} %get-tuple-element.272, f32[]{:T(128)S(6)} %rsqrt.263, ...), kind=kLoop, calls=%fused_computation.342 | loop fusion | flops 20160 | bytes 19340 | tf_op jit(solution)/shard_map/mul | solution.py:35
  1109.5 71.6 %all-reduce.7.cloned.1.call-done = (bf16[1,1280,8]{1,2,0:T(8,128)(2,1)}, bf16[1,1280,8]{1,2,0:T(8,128)(2,1)}, bf16[1,1280,8]{1,2,0:T(8,128)(2,1)}, bf16[1,1280,8...) async-done(((bf16[1,1280,8]{1,2,0:T(8,128)(2,1)}, bf16[1,1280,8]{1,2,0:T(8,128)(2,1)}, bf16[1,1280,8]{1,2,0:T(8,128)(2,1)}, ...) | async-done | bytes 122896 | tf_op jit(solution)/shard_map/psum | solution.py:206
  1185.5 12.8 %bitcast_subtract_fusion = (f32[320,6,1280]{2,0,1:T(8,128)}, f32[6,1280,320]{1,2,0:T(8,128)S(1)}) fusion(f32[320,6,1280]{2,0,1:T(8,128)} %convert_add_fusion, f32[6,1280,8]{1,2,0:T(8,128)S(1)} %convert_multiply_fusion.5, f32[320,6,8]{0,2,1:T(8,128)S(1)} %constant_dynamic-update-slice_fusion.8), kind=kOutput, calls=%fused_computation.7 | convolution fusion | flops 238387200 | bytes 29798400 | tf_op jit(solution)/shard_map/upt,pqt->upq/dot_general | solution.py:211
  (296 shorter events, 357.4 us)
Async XLA Ops:
  7.2 648.8 %copy-start = (f32[6,1280,8]{1,2,0:T(8,128)S(1)}, f32[6,1280,8]{1,2,0:T(8,128)}, u32[]{:S(2)}) copy-start(f32[6,1280,8]{1,2,0:T(8,128)} %param.14) | copy-start | bytes 737284
  7.2 7.8 copy-start.1
  7.2 129.4 %all-gather.7.cloned.1.call-start = ((), (), s32[]{:S(2)}) async-start(), calls=%async_computation.4 | async-start | bytes 24576000 | tf_op jit(solution)/shard_map/all_gather | solution.py:62
  7.9 167.5 %all-gather.9.cloned.1.call-start = ((), (), s32[]{:S(2)}) async-start(), calls=%async_computation.7 | async-start | bytes 3276800 | tf_op jit(solution)/shard_map/all_gather | solution.py:83
  14.3 132.7 %copy-start.25 = (f32[1280,5]{0,1:T(8,128)}, f32[1280,5]{0,1:T(8,128)S(1)}, u32[]{:S(2)}) copy-start(f32[1280,5]{0,1:T(8,128)S(1)} %reshape.8102) | copy-start | bytes 76804
  15.0 136.4 %copy-start.26 = (f32[1280]{0:T(1024)}, f32[1280]{0:T(1024)S(1)}, u32[]{:S(2)}) copy-start(f32[1280]{0:T(1024)S(1)} %get-tuple-element.55) | copy-start | bytes 15364
  15.0 138.7 %copy-start.22 = (f32[1280]{0:T(1024)}, f32[1280]{0:T(1024)S(1)}, u32[]{:S(2)}) copy-start(f32[1280]{0:T(1024)S(1)} %get-tuple-element.58) | copy-start | bytes 15364
  15.8 137.9 %copy-start.28 = (f32[384]{0:T(512)}, f32[384]{0:T(512)S(1)}, u32[]{:S(2)}) copy-start(f32[384]{0:T(512)S(1)} %get-tuple-element.453) | copy-start | bytes 4612
  149.7 53.4 %all-gather.11.cloned.1.call-start = ((), (), s32[]{:S(2)}) async-start(), calls=%async_computation.8 | async-start | bytes 3276800 | tf_op jit(solution)/shard_map/all_gather | solution.py:82
  150.5 248.2 %reduce-scatter.9.cloned.1.call-start = ((), (), s32[]{:S(2)}) async-start(), calls=%async_computation.5 | async-start | bytes 3276800 | tf_op jit(solution)/shard_map/reduce_scatter | solution.py:155
  218.6 13.1 %copy-start.3 = (pred[384,1152]{1,0:T(8,128)(4,1)S(1)}, pred[384,1152]{1,0:T(8,128)(4,1)}, u32[]{:S(2)}) copy-start(pred[384,1152]{1,0:T(8,128)(4,1)} %fusion.50) | copy-start | bytes 1327108
  231.6 13.7 %copy-start.2 = (bf16[1152,1280]{0,1:T(8,128)(2,1)S(1)}, bf16[1152,1280]{0,1:T(8,128)(2,1)}, u32[]{:S(2)}) copy-start(bf16[1152,1280]{0,1:T(8,128)(2,1)} %copy.80) | copy-start | bytes 8847364
  264.9 16.4 %copy-start.9 = (f32[384,1280]{1,0:T(8,128)}, f32[384,1280]{1,0:T(8,128)S(1)}, u32[]{:S(2)}) copy-start(f32[384,1280]{1,0:T(8,128)S(1)} %get-tuple-element.461) | copy-start | bytes 5898244
  271.7 5.0 copy-start.42
  354.0 71.6 %reduce-scatter.11.cloned.1.call-start = ((), (), s32[]{:S(2)}) async-start(), calls=%async_computation.6 | async-start | bytes 3276800 | tf_op jit(solution)/shard_map/reduce_scatter | solution.py:158
  376.2 119.9 %reduce-scatter.15.cloned.1.call-start = ((), (), s32[]{:S(2)}) async-start(), calls=%async_computation.10 | async-start | bytes 819200
  392.5 4.8 copy-start.27
  397.3 28.3 %copy-start.14 = (bf16[1,128,1280]{2,1,0:T(8,128)(2,1)S(1)}, bf16[1,128,1280]{2,1,0:T(8,128)(2,1)}, u32[]{:S(2)}) copy-start(bf16[1,128,1280]{2,1,0:T(8,128)(2,1)} %copy.88) | copy-start | bytes 983044
  398.7 29.2 %copy-start.6 = (f32[384,1280]{1,0:T(8,128)S(1)}, f32[384,1280]{1,0:T(8,128)}, u32[]{:S(2)}) copy-start(f32[384,1280]{1,0:T(8,128)} %copy-done.5) | copy-start | bytes 5898244
  431.0 9.2 copy-start.30
  442.1 187.0 %reduce-scatter.13.cloned.1.call-start = ((), (), s32[]{:S(2)}) async-start(), calls=%async_computation.9 | async-start | bytes 24576000
  486.4 252.5 %all-reduce.5.cloned.1.call-start = ((), (), s32[]{:S(2)}) async-start(), calls=%async_computation.11 | async-start | bytes 172032 | tf_op jit(solution)/shard_map/psum | solution.py:201
  656.0 11.7 copy-start.37
  667.3 513.8 %all-reduce.7.cloned.1.call-start = ((), (), s32[]{:S(2)}) async-start(), calls=%async_computation.12 | async-start | bytes 245760 | tf_op jit(solution)/shard_map/psum | solution.py:206
  739.0 124.4 %copy-start.34 = (f32[320,8]{0,1:T(8,128)S(1)}, f32[320,8]{0,1:T(8,128)}, u32[]{:S(2)}) copy-start(f32[320,8]{0,1:T(8,128)} %get-tuple-element.223) | copy-start | bytes 30724
  798.1 126.5 %copy-start.33 = (f32[320,8]{0,1:T(8,128)S(1)}, f32[320,8]{0,1:T(8,128)}, u32[]{:S(2)}) copy-start(f32[320,8]{0,1:T(8,128)} %get-tuple-element.224) | copy-start | bytes 30724
  860.3 125.8 %copy-start.32 = (f32[320,8]{0,1:T(8,128)S(1)}, f32[320,8]{0,1:T(8,128)}, u32[]{:S(2)}) copy-start(f32[320,8]{0,1:T(8,128)} %get-tuple-element.225) | copy-start | bytes 30724
  921.6 125.8 %copy-start.31 = (f32[320,8]{0,1:T(8,128)S(1)}, f32[320,8]{0,1:T(8,128)}, u32[]{:S(2)}) copy-start(f32[320,8]{0,1:T(8,128)} %get-tuple-element.226) | copy-start | bytes 30724
  983.0 125.8 %copy-start.35 = (f32[5,320]{1,0:T(8,128)S(1)}, f32[5,320]{1,0:T(8,128)}, u32[]{:S(2)}) copy-start(f32[5,320]{1,0:T(8,128)} %param.16) | copy-start | bytes 19204
  983.1 125.8 %copy-start.36 = (f32[5,320]{1,0:T(8,128)S(1)}, f32[5,320]{1,0:T(8,128)}, u32[]{:S(2)}) copy-start(f32[5,320]{1,0:T(8,128)} %get-tuple-element.227) | copy-start | bytes 19204
  1185.5 12.9 %copy-start.16 = (f32[6,1280,8]{1,2,0:T(8,128)}, f32[6,1280,8]{1,2,0:T(8,128)S(1)}, u32[]{:S(2)}) copy-start(f32[6,1280,8]{1,2,0:T(8,128)S(1)} %convert_multiply_fusion.5) | copy-start | bytes 737284
  1185.5 12.8 %copy-start.8 = (f32[320,6,160]{2,0,1:T(8,128)S(1)}, f32[320,6,160]{2,0,1:T(8,128)}, u32[]{:S(2)}) copy-start(f32[320,6,160]{2,0,1:T(8,128)} %copy.92) | copy-start | bytes 3686404
  (21 other events, 59.8 us)
Sparse Core Ops, SparseCore 0:
  9.6 126.9 all-gather.6
  149.9 25.5 all-gather.8
  177.6 25.5 all-gather.10
  354.1 34.4 reduce-scatter.8
  391.1 34.5 reduce-scatter.10
  442.2 22.4 reduce-scatter.14
  486.6 142.4 reduce-scatter.12
  667.5 71.4 all-reduce.4
  1109.6 71.4 all-reduce.6
where the time goes:
time: 1230 us; the launch traced here: 1220 us
  waiting for transfers between devices  457 us (37%)
  other arithmetic  393 us (32%)
  matrix products  192 us (16%)
  local copies, waits for them, and re-layouts  118 us (10%)
  between operations  47.3 us (4%)
    reduce_sum x60, other arithmetic, orthonormal(): jnp.sum(earlier * column, axis=-2, keepdims=True) * earlier  164 us
    unnamed x11, waiting for transfers between devices  133 us
    all_gather x1, waiting for transfers between devices, on_device(): lax.all_gather(weights, 'zero', axis=0, tiled=True)  121 us
    mul x6, other arithmetic, orthonormal(): column * lax.rsqrt(jnp.sum(column * column, axis=-2, keepdims=True) + EPS)  106 us
    psum x1, waiting for transfers between devices, on_device(): lax.psum(right_term.astype(jnp.bfloat16), 'rep').astype(jnp.float32)  71.6 us
    psum x1, waiting for transfers between devices, on_device(): left_sum = lax.psum(local_left_factor[:, mat_index], 'rep')  68 us
    unnamed x106, local copies, waits for them, and re-layouts  62 us
    reduce_sum x30, other arithmetic, orthonormal(): jnp.sum(column * column, axis=-2, keepdims=True) + EPS  49.2 us
  transfers between devices with their start and end apart: 9, of which 7 were waited for; matrix products, arithmetic and copies ran while one was open for 9% of the time, Pallas kernels for 0%

commit v1 on v0

v1 whole, which is shorter than its diff:
```python
import math

import jax
import jax.numpy as jnp
from jax import lax
from jax.experimental import pallas as pl
from jax.experimental.pallas import tpu as pltpu
from jax.sharding import PartitionSpec as P

HEADS = 16
PROMPT = 1024
LANES = 128

EPS = 1e-06
MU = 0.9
LOG2E = 1.442695041
NEG = -1e30
PRECISION_HIGH = lax.Precision.HIGHEST
f32 = jnp.float32
bf16 = jnp.bfloat16


def rms_scale(field):
    return lax.rsqrt(jnp.mean(field * field, axis=-1, keepdims=True) + EPS)


def norm_back(field, scale, gain_vec, grad_in):
    weighted = grad_in * gain_vec
    inner = jnp.mean(field * weighted, axis=-1, keepdims=True)
    return scale * weighted - field * (scale * scale * scale) * inner


def to_pair(x, count):
    return lax.ppermute(x, "zero", [(i, i ^ 1) for i in range(count)])


def to_chip(x, count, shift):
    return lax.ppermute(x, "zero", [(i, (i + 2 * shift) % count) for i in range(count)])


def place(buffer, block, index):
    starts = (index,) + (0,) * block.ndim
    return lax.dynamic_update_slice(buffer, block[None], starts)


def gather_zero(x, index, count):
    chip, core = index // 2, index % 2
    chips = count // 2
    out = jnp.zeros((count,) + x.shape, x.dtype)
    for shift in range(chips):
        block = x if shift == 0 else to_chip(x, count, shift)
        owner = (chip - shift + chips) % chips
        out = place(out, block, owner * 2 + core)
        out = place(out, to_pair(block, count), owner * 2 + 1 - core)
    return out


def scatter_sum_zero(y, index, count, dtype):
    chip, core = index // 2, index % 2
    chips = count // 2
    paired = y.reshape((chips, 2) + y.shape[1:])
    away = lax.dynamic_index_in_dim(paired, 1 - core, 1, keepdims=False)
    mine = lax.dynamic_index_in_dim(paired, core, 1, keepdims=False)
    mine = mine.astype(f32) + to_pair(away, count).astype(f32)
    total = lax.dynamic_index_in_dim(mine, chip, 0, keepdims=False)
    for shift in range(1, chips):
        sent = lax.dynamic_index_in_dim(mine, (chip + shift) % chips, 0, keepdims=False)
        total = total + to_chip(sent.astype(dtype), count, shift).astype(f32)
    return total


def exchange_zero(y, index, count):
    chip, core = index // 2, index % 2
    chips = count // 2
    by_chip = y.reshape((chips, 2) + y.shape[1:])
    out = jnp.zeros(y.shape, y.dtype)
    for shift in range(chips):
        sent = lax.dynamic_index_in_dim(by_chip, (chip + shift) % chips, 0, keepdims=False)
        held = sent if shift == 0 else to_chip(sent, count, shift)
        source = (chip - shift + chips) % chips
        own = lax.dynamic_index_in_dim(held, core, 0, keepdims=False)
        other = lax.dynamic_index_in_dim(held, 1 - core, 0, keepdims=False)
        out = place(out, own, source * 2 + core)
        out = place(out, to_pair(other, count), source * 2 + 1 - core)
    return out


def sum_rep(x, count, dtype=f32):
    step = 1
    while step < count:
        low = x.astype(dtype)
        far = lax.ppermute(low, "rep", [(i, i ^ step) for i in range(count)])
        x = low.astype(f32) + far.astype(f32)
        step *= 2
    return x


def ortho_body(left_ref, out_ref):
    rank = left_ref.shape[0]
    columns = [left_ref[c] for c in range(rank)]
    for e in range(rank):
        done = columns[e]
        done = done * lax.rsqrt(jnp.sum(done * done, axis=-1, keepdims=True) + EPS)
        out_ref[e] = done
        for c in range(e + 1, rank):
            columns[c] = columns[c] - jnp.sum(done * columns[c], axis=-1, keepdims=True) * done


def orthonormal(left):
    return pl.pallas_call(
        ortho_body, out_shape=jax.ShapeDtypeStruct(left.shape, f32), name="ortho"
    )(left)


def on_device(
    tokens,
    cotangent,
    weights,
    vectors,
    error,
    previous_right_factors,
    momentum,
    vec_momentum,
    prompt_len,
):
    zero_index = lax.axis_index("zero")
    rep_index = lax.axis_index("rep")
    n = lax.axis_size("zero")
    rep_count = lax.axis_size("rep")
    rows, width = tokens.shape
    head_dim = width // HEADS
    heads = HEADS // n
    own = weights.shape[0]
    group_rows = n * rows
    prompt_rows = PROMPT // n
    prompt_valid = prompt_len[0]

    full_v = gather_zero(vectors, zero_index, n).transpose(1, 0, 2).reshape(5, width)
    vec_float = full_v.astype(f32)
    gain_one, gain_two, bias_one, bias_two = (vec_float[i] for i in range(4))
    scale_raw = vectors[4].astype(f32)
    far_w = gather_zero(weights[:, 3:6, :], zero_index, n).reshape(width, 3, width)

    tok_all = gather_zero(tokens, zero_index, n).reshape(group_rows, width)
    tok_all_float = tok_all.astype(f32)
    normed_all = (tok_all_float * rms_scale(tok_all_float) * gain_one).astype(bf16)

    projected = jnp.einsum(
        "ti,omi->mto", normed_all, weights[:, 0:3, :], preferred_element_type=f32
    )
    scale_const = LOG2E / math.sqrt(head_dim)
    query_scale = scale_const * jax.nn.softplus(scale_raw)
    query = projected[0]
    scaled = (query * query_scale).astype(bf16).reshape(group_rows, heads, head_dim)
    key_low = projected[1].astype(bf16).reshape(group_rows, heads, head_dim)
    value_low = projected[2].astype(bf16).reshape(group_rows, heads, head_dim)

    index = jnp.arange(group_rows, dtype=jnp.int32)
    block, offset = index // rows, index % rows
    is_prompt = offset < prompt_rows
    pos = block * prompt_rows + offset
    see_prompt = (is_prompt & (pos < prompt_valid))[None] & (
        jnp.logical_not(is_prompt)[:, None] | (pos[None] <= pos[:, None])
    )
    see_cont = (
        jnp.logical_not(is_prompt)[None]
        & jnp.logical_not(is_prompt)[:, None]
        & (block[None] == block[:, None])
        & (offset[None] <= offset[:, None])
    )
    allowed = see_prompt | see_cont

    def masked_scores():
        raw = jnp.einsum("thd,khd->htk", scaled, key_low, preferred_element_type=f32)
        return jnp.where(allowed[None], raw, NEG)

    masked = masked_scores()
    row_top = jnp.max(masked, axis=-1, keepdims=True)
    log_total = row_top + jnp.log(jnp.sum(jnp.exp(masked - row_top), axis=-1, keepdims=True))
    probs = jnp.exp(masked - log_total)
    attended_heads = jnp.einsum(
        "htk,khd->thd", probs.astype(bf16), value_low, preferred_element_type=f32
    ).astype(bf16)
    attended = (
        exchange_zero(attended_heads.reshape(n, rows, own), zero_index, n)
        .transpose(1, 0, 2)
        .reshape(rows, width)
    )

    tok_float = tokens.astype(f32)
    scale_one = rms_scale(tok_float)
    hidden = tok_float + jnp.einsum("ti,oi->to", attended, far_w[:, 0], preferred_element_type=f32)
    scale_two = rms_scale(hidden)
    normed_two = (hidden * scale_two * gain_two).astype(bf16)
    upper = (
        jnp.einsum("ti,oi->to", normed_two, far_w[:, 1], preferred_element_type=f32) + bias_one
    )
    activ = jax.nn.silu(upper).astype(bf16)
    output = jnp.einsum("ti,oi->to", activ, far_w[:, 2], preferred_element_type=f32) + bias_two
    result = (hidden + output).astype(bf16)

    grad_out = cotangent.astype(f32)
    grad_f = cotangent.astype(bf16)
    grad_act = jnp.einsum("to,oi->ti", grad_f, far_w[:, 2], preferred_element_type=f32)
    gate_sig = jax.nn.sigmoid(upper)
    grad_up = (grad_act * gate_sig * (1.0 + upper * (1.0 - gate_sig))).astype(bf16)
    grad_n2 = jnp.einsum("to,oi->ti", grad_up, far_w[:, 1], preferred_element_type=f32)
    grad_gain_two = jnp.sum(grad_n2 * hidden * scale_two, axis=0)
    grad_hidden = grad_out + norm_back(hidden, scale_two, gain_two, grad_n2)
    grad_branch = grad_hidden.astype(bf16)
    grad_att = jnp.einsum(
        "to,oi->ti", grad_branch, far_w[:, 0], preferred_element_type=f32
    ).astype(bf16)
    grad_att_heads = exchange_zero(
        grad_att.reshape(rows, n, own).transpose(1, 0, 2), zero_index, n
    ).reshape(group_rows, heads, head_dim)

    far_grads = jnp.einsum(
        "mto,mti->omi",
        jnp.stack([grad_branch, grad_up, grad_f], axis=0),
        jnp.stack([attended, normed_two, activ], axis=0),
        preferred_element_type=f32,
    ).astype(bf16)
    far_block = scatter_sum_zero(far_grads.reshape(n, own, 3, width), zero_index, n, bf16)

    probs_again = jnp.exp(masked_scores() - log_total)
    grad_probs = jnp.einsum("thd,khd->htk", grad_att_heads, value_low, preferred_element_type=f32)
    delta = jnp.sum(probs_again * grad_probs, axis=-1, keepdims=True)
    grad_scores = (probs_again * (grad_probs - delta)).astype(bf16)
    grad_value = jnp.einsum(
        "htk,thd->khd", probs_again.astype(bf16), grad_att_heads, preferred_element_type=f32
    ).reshape(group_rows, own)
    grad_key = jnp.einsum(
        "htk,thd->khd", grad_scores, scaled, preferred_element_type=f32
    ).reshape(group_rows, own)
    grad_sq = jnp.einsum("htk,khd->thd", grad_scores, key_low, preferred_element_type=f32).reshape(
        group_rows, own
    )
    grad_query = grad_sq * query_scale
    grad_proj = jnp.stack([grad_query, grad_key, grad_value], axis=0).astype(bf16)
    near_block = jnp.einsum("mto,ti->omi", grad_proj, normed_all, preferred_element_type=f32)
    grad_n1_part = jnp.einsum(
        "mto,omi->ti", grad_proj, weights[:, 0:3, :], preferred_element_type=f32
    ).astype(bf16)
    grad_n1 = scatter_sum_zero(grad_n1_part.reshape(n, rows, width), zero_index, n, bf16)
    grad_tokens = grad_hidden + norm_back(tok_float, scale_one, gain_one, grad_n1)

    grad_scale_raw = jnp.sum(grad_sq * query, axis=0) * scale_const * jax.nn.sigmoid(scale_raw)
    vec_terms = jnp.stack(
        [
            jnp.sum(grad_n1 * tok_float * scale_one, axis=0),
            grad_gain_two,
            jnp.sum(grad_up.astype(f32), axis=0),
            jnp.sum(grad_f.astype(f32), axis=0),
        ],
        axis=0,
    )
    vec_block = scatter_sum_zero(
        vec_terms.reshape(4, n, own).transpose(1, 0, 2), zero_index, n, f32
    )
    vec_total = sum_rep(jnp.concatenate([vec_block, grad_scale_raw[None]], axis=0), rep_count)

    merged = jnp.concatenate([near_block, far_block], axis=1) + error
    left = jnp.einsum("omi,mir->rmo", merged, previous_right_factors, precision=PRECISION_HIGH)
    ortho = orthonormal(sum_rep(left, rep_count) / rep_count)
    right = jnp.einsum("omi,rmo->rmi", merged, ortho, precision=PRECISION_HIGH)
    right = sum_rep(right, rep_count, bf16) / rep_count
    fresh_right_factors = right.transpose(1, 2, 0)
    approximation = jnp.einsum("rmo,rmi->omi", ortho, right, precision=PRECISION_HIGH)
    new_error = merged - approximation

    rep_width = width // rep_count
    grad_weights = lax.dynamic_slice_in_dim(approximation, rep_index * rep_width, rep_width, 2)
    step_rate = 0.03 / math.sqrt(group_rows)
    new_momentum = MU * momentum + grad_weights
    update_weights = -step_rate * new_momentum
    grad_vectors = vec_total / rep_count
    new_vec_momentum = MU * vec_momentum + grad_vectors
    update_vectors = -step_rate * new_vec_momentum
    return (
        result,
        grad_tokens,
        grad_weights,
        grad_vectors,
        new_error,
        fresh_right_factors,
        new_momentum,
        new_vec_momentum,
        update_weights,
        update_vectors,
    )


def solution(mesh):
    in_specs = (
        P(("rep", "zero"), None),
        P(("rep", "zero"), None),
        P("zero", None, None),
        P(None, "zero"),
        P(("rep", "zero"), None, None),
        P(None, None, "zero"),
        P("zero", None, "rep"),
        P(None, "zero"),
        P("rep"),
    )
    out_specs = (
        P(("rep", "zero"), None),
        P(("rep", "zero"), None),
        P("zero", None, "rep"),
        P(None, "zero"),
        P(("rep", "zero"), None, None),
        P(None, None, "zero"),
        P("zero", None, "rep"),
        P(None, "zero"),
        P("zero", None, "rep"),
        P(None, "zero"),
    )
    return jax.shard_map(
        on_device, mesh=mesh, in_specs=in_specs, out_specs=out_specs, check_vma=False
    )
```

time: 1230 us -> 498 us (0.40)
  waiting for transfers between devices: 457 us -> 90.8 us
  other arithmetic: 393 us -> 89.2 us
  between operations: 47.3 us -> 3.13 us
  starting transfers between devices: 0.83 us -> 30.1 us
  local copies, waits for them, and re-layouts: 118 us -> 91 us
    reduce_sum x91 -> x1, other arithmetic: 213 us -> 0.72 us  [on_device(): jnp.sum(grad_n1 * tok_float * scale_one, axis=0)]
    all_gather x3 -> x0, waiting for transfers between devices: 161 us -> none  [the longest x1 121 us: on_device(): lax.all_gather(weights, 'zero', axis=0, tiled=True)]
    psum x2 -> x0, waiting for transfers between devices: 140 us -> none  [the longest x1 71.6 us: on_device(): lax.psum(right_term.astype(jnp.bfloat16), 'rep').astype(jnp.float32)]
    unnamed x11 -> x0, waiting for transfers between devices: 133 us -> none
    mul x6 -> x1, other arithmetic: 106 us -> 0.04 us  [on_device(): query_scale = scale_const * jax.nn.softplus(scale_raw)]
    ppermute x0 -> x30, waiting for transfers between devices: none -> 90.8 us  [the longest x8 75.1 us: to_chip(): lax.ppermute(x, 'zero', [(i, (i + 2 * shift) % count) for i in range(coun...]
    unnamed x106 -> x108, local copies, waits for them, and re-layouts: 62 us -> 16.5 us
    ppermute x0 -> x30, starting transfers between devices: none -> 30.1 us  [the longest x9 17.9 us: sum_rep(): far = lax.ppermute(low, 'rep', [(i, i ^ step) for i in range(count)])]
  transfers between devices with their start and end apart: 9 -> 30, of which waited for: 7 -> 10; matrix products, arithmetic and copies ran while one was open for 9% -> 55% of each run, Pallas kernels for 0% -> 1%
where the time goes in v1:
time: 498 us; the launch traced here: 495 us
  matrix products  188 us (38%)
  local copies, waits for them, and re-layouts  91 us (18%)
  waiting for transfers between devices  90.8 us (18%)
  other arithmetic  89.2 us (18%)
  starting transfers between devices  30.1 us (6%)
    ppermute x8, waiting for transfers between devices, to_chip(): lax.ppermute(x, 'zero', [(i, (i + 2 * shift) % count) for i in range(coun...  75.1 us
    convert_element_type x1, other arithmetic, on_device(): grad_scores = (probs_again * (grad_probs - delta)).astype(bf16)  31.7 us
    dot_general x1, matrix products, on_device(): jnp.einsum('thd,khd->htk', grad_att_heads, value_low, preferred_element_t...  28.6 us
    dynamic_update_slice x19, local copies, waits for them, and re-layouts, place(): return lax.dynamic_update_slice(buffer, block[None], starts)  25.1 us
    ppermute x9, starting transfers between devices, sum_rep(): far = lax.ppermute(low, 'rep', [(i, i ^ step) for i in range(count)])  17.9 us
    dot_general x1, matrix products, masked_scores(): jnp.einsum('thd,khd->htk', scaled, key_low, preferred_element_type=f32)  16.7 us
    unnamed x108, local copies, waits for them, and re-layouts  16.5 us
    dot_general x1, matrix products, on_device(): jnp.einsum('htk,thd->khd', probs_again.astype(bf16), grad_att_heads, pref...  16.2 us
  transfers between devices with their start and end apart: 30, of which 10 were waited for; matrix products, arithmetic and copies ran while one was open for 55% of the time, Pallas kernels for 1%

profile of v1, /device:TPU:0, one launch (start us, length us, event | category | flops | bytes accessed | tf_op | source)
XLA Modules:
  0.0 494.8 jit_solution(9915052075028006674)
XLA Ops:
  12.4 4.7 broadcast_in_dim.114
  19.4 6.1 %and_or_fusion = pred[1536,1536]{0,1:T(8,128)(4,1)} fusion(s32[1536]{0:T(1024)S(1)} %get-tuple-element.88, s32[1536]{0:T(1024)S(1)} %get-tuple-element.87, s32[1536]{0:T(1024)S(1)} %multiply_add_fusion.2, pred[1536]{0:T(1024)(128)(4,1)S(1)} %get-tuple-element.89, pred[1536]{0:T(1024)(128)(4,1)S(1)} %get-tuple-element.90), kind=kLoop, calls=%fused_computation.10 | loop fusion | flops 21233664 | bytes 2380800 | tf_op jit(solution)/shard_map/or | solution.py:171
  41.5 4.0 fusion.79
  45.8 16.7 %fusion.80 = (f32[4,1536]{1,0:T(4,128)S(1)}, f32[4,1536,1536]{1,2,0:T(8,128)}) fusion(bf16[1536,4,80]{0,2,1:T(8,128)(2,1)S(1)} %bitcast.237, f32[1536,4,80]{0,2,1:T(8,128)S(1)} %bitcast.230, f32[4,80]{1,0:T(4,128)S(1)} %mul.311, pred[1536,1536]{0,1:T(8,128)(4,1)} %and_or_fusion), kind=kOutput, calls=%fused_computation.194 | convolution fusion | flops 1529800704 | bytes 43083008 | tf_op jit(solution)/shard_map/thd,khd->htk/dot_general | solution.py:174
  62.6 14.9 %exponential_reduce_fusion = f32[4,1536]{1,0:T(4,128)S(1)} fusion(f32[4,1536,1536]{1,2,0:T(8,128)} %get-tuple-element.75, f32[4,1536]{1,0:T(4,128)S(1)} %get-tuple-element.74), kind=kLoop, calls=%fused_computation.4 | loop fusion | flops 18868224 | bytes 37797888 | tf_op jit(solution)/shard_map/reduce_sum | solution.py:179
  77.5 5.8 %collective-permute-done.10 = bf16[320,3,1280]{2,0,1:T(8,128)(2,1)} collective-permute-done((bf16[320,3,1280]{2,0,1:T(8,128)(2,1)}, bf16[320,3,1280]{2,0,1:T(8,128)(2,1)}, u32[]{:S(2)}, u32[]{:S(2)}) %collective-permute-start.10) | collective-permute-done | bytes 2457632 | tf_op jit(solution)/shard_map/ppermute | solution.py:38
  83.3 16.0 %fusion.34 = bf16[1536,4,80]{0,2,1:T(8,128)(2,1)} fusion(bf16[1536,4,80]{0,2,1:T(8,128)(2,1)S(1)} %bitcast.240, f32[4,1536,1536]{1,2,0:T(8,128)} %get-tuple-element.75, f32[4,1536]{1,0:T(4,128)S(1)} %log_add_fusion), kind=kOutput, calls=%fused_computation.61 | convolution fusion | flops 1529315328 | bytes 39739392 | tf_op jit(solution)/shard_map/htk,khd->thd/dot_general | solution.py:181
  114.6 5.6 %collective-permute-done.7 = bf16[2,384,320]{1,2,0:T(8,128)(2,1)S(1)} collective-permute-done((bf16[2,384,320]{1,2,0:T(8,128)(2,1)S(1)}, bf16[2,384,320]{1,2,0:T(8,128)(2,1)S(1)}, u32[]{:S(2)}, u32[]{:S(2)}) %collective-permute-start.7) | collective-permute-done | bytes 491552 | tf_op jit(solution)/shard_map/ppermute | solution.py:38
  130.9 3.8 multiply_reduce_fusion.4
  134.7 4.1 convolution_add_fusion.1
  138.9 4.4 convert_reduce_fusion.1
  143.3 3.9 multiply_reduce_fusion.2
  150.7 4.3 fusion.25
  164.5 4.7 fusion.27
  171.2 11.0 %convolution_convert_fusion = bf16[3,1280,1280]{1,2,0:T(8,128)(2,1)} fusion(bf16[1,384,1280]{2,1,0:T(8,128)(2,1)} %fusion.76, bf16[1,384,1280]{2,1,0:T(8,128)(2,1)} %get-tuple-element.60, bf16[1,384,1280]{2,1,0:T(8,128)(2,1)S(1)} %copy-done.25, bf16[1,384,1280]{2,1,0:T(8,128)(2,1)S(1)} %bitcast.251, bf16[1,384,1280]{2,1,0:T(8,128)(2,1)} %bitcast.261, ...), kind=kOutput, calls=%fused_computation.6 | convolution fusion | flops 3785687040 | bytes 15728640 | tf_op jit(solution)/shard_map/mto,mti->omi/dot_general | solution.py:218
  187.8 8.2 %constant_dynamic-slice_fusion.2 = (bf16[2,1,320,3,1280]{4,2,1,0,3:T(8,128)(2,1)}, bf16[2,1,320,3,1280]{4,2,1,0,3:T(8,128)(2,1)}) fusion(bf16[2,2,320,3,1280]{4,2,1,0,3:T(8,128)(2,1)} %bitcast.239, s32[]{:T(128)S(6)} %select_n.237, s32[]{:T(128)S(6)} %select_n.239), kind=kLoop, calls=%fused_computation.144 | loop fusion | bytes 19660808 | tf_op jit(solution)/shard_map/jit(dynamic_index_in_dim)/dynamic_slice | solution.py:63
  196.0 5.0 %copy.110 = bf16[2,1,320,3,1280]{4,2,3,0,1:T(8,128)(2,1)} copy(bf16[2,1,320,3,1280]{4,2,1,0,3:T(8,128)(2,1)} %get-tuple-element.57) | data formatting | bytes 9830400 | tf_op jit(solution)/shard_map/jit(dynamic_index_in_dim)/dynamic_slice | solution.py:62
  207.6 28.6 %multiply_reduce_fusion = (f32[4,1536]{1,0:T(4,128)S(1)}, f32[4,1536,1536]{1,2,0:T(8,128)}) fusion(f32[4,1536,1536]{1,2,0:T(8,128)} %get-tuple-element.75, f32[4,1536]{1,0:T(4,128)S(1)} %log_add_fusion, bf16[1536,4,80]{0,2,1:T(8,128)(2,1)} %reshape.403, bf16[1536,4,80]{0,2,1:T(8,128)(2,1)} %bitcast.241), kind=kOutput, calls=%fused_computation.2 | convolution fusion | flops 1538254848 | bytes 77512704 | tf_op jit(solution)/shard_map/thd,khd->htk/dot_general | solution.py:227
  236.2 31.7 %multiply_convert_fusion = bf16[4,1536,1536]{1,2,0:T(8,128)(2,1)} fusion(f32[4,1536,1536]{1,2,0:T(8,128)} %get-tuple-element.80, f32[4,1536,1536]{1,2,0:T(8,128)} %get-tuple-element.75, f32[4,1536]{1,0:T(4,128)S(1)} %get-tuple-element.79, f32[4,1536]{1,0:T(4,128)S(1)} %log_add_fusion), kind=kLoop, calls=%fused_computation.1 | loop fusion | flops 37748736 | bytes 94420992 | tf_op jit(solution)/shard_map/convert_element_type | solution.py:229
  267.9 8.2 %fusion.49 = (f32[4,80]{1,0:T(4,128)S(1)}, f32[4,80,1536]{2,1,0:T(8,128)S(1)}) fusion(f32[1536,4,80]{0,2,1:T(8,128)S(1)} %bitcast.231, bf16[1536,4,80]{0,2,1:T(8,128)(2,1)S(1)} %bitcast.238, bf16[4,1536,1536]{1,2,0:T(8,128)(2,1)} %multiply_convert_fusion), kind=kOutput, calls=%fused_computation.84 | convolution fusion | flops 1510932224 | bytes 23790848 | tf_op jit(solution)/shard_map/htk,khd->thd/dot_general | solution.py:236
  277.3 10.8 %convolution_convert_fusion.1 = bf16[4,80,1536]{2,1,0:T(8,128)(2,1)} fusion(bf16[4,1536,1536]{1,2,0:T(8,128)(2,1)} %multiply_convert_fusion, f32[1536,4,80]{0,2,1:T(8,128)S(1)} %bitcast.232, f32[4,80]{1,0:T(4,128)S(1)} %mul.311), kind=kOutput, calls=%fused_computation.60 | convolution fusion | flops 1511424000 | bytes 21824768 | tf_op jit(solution)/shard_map/htk,thd->khd/dot_general | solution.py:233
  288.1 16.2 %fusion.31 = bf16[4,80,1536]{2,1,0:T(8,128)(2,1)} fusion(bf16[1536,4,80]{0,2,1:T(8,128)(2,1)S(1)} %copy-done.8, f32[4,1536,1536]{1,2,0:T(8,128)} %get-tuple-element.75, f32[4,1536]{1,0:T(4,128)S(1)} %log_add_fusion), kind=kOutput, calls=%fused_computation.59 | convolution fusion | flops 1529315328 | bytes 39739392 | tf_op jit(solution)/shard_map/htk,thd->khd/dot_general | solution.py:230
  304.2 6.3 %fusion.3 = bf16[1536,1280]{1,0:T(8,128)(2,1)S(1)} fusion(bf16[320,6,1280]{2,0,1:T(8,128)(2,1)} %param.11, bf16[1,1536,320]{1,2,0:T(8,128)(2,1)} %bitcast.254, bf16[1,1536,320]{1,2,0:T(8,128)(2,1)S(1)} %bitcast.252, bf16[1,1536,320]{1,2,0:T(8,128)(2,1)S(1)} %copy-done.26), kind=kOutput, calls=%fused_computation.16 | convolution fusion | flops 3779788800 | bytes 9338880 | tf_op jit(solution)/shard_map/mto,omi->ti/dot_general | solution.py:242
  313.7 5.0 %convert_add_fusion = f32[2,320,3,1280]{3,1,2,0:T(8,128)S(1)} fusion(bf16[2,320,3,1280]{3,1,2,0:T(8,128)(2,1)} %collective-permute-done.17, bf16[2,1,320,3,1280]{4,2,1,0,3:T(8,128)(2,1)} %get-tuple-element.56), kind=kLoop, calls=%fused_computation.8 | loop fusion | flops 7372800 | bytes 19660800 | tf_op jit(solution)/shard_map/add | solution.py:64
  327.9 5.8 %convolution_bitcast_fusion.2 = f32[320,3,1280]{2,0,1:T(8,128)} fusion(bf16[1536,1280]{1,0:T(8,128)(2,1)S(1)} %copy-done.13, bf16[1,1536,320]{1,2,0:T(8,128)(2,1)S(1)} %bitcast.255, bf16[1,1536,320]{1,2,0:T(8,128)(2,1)S(1)} %bitcast.253, bf16[1,1536,320]{1,2,0:T(8,128)(2,1)S(1)} %copy-done.27), kind=kOutput, calls=%fused_computation.24 | convolution fusion | flops 3783720960 | bytes 11796480 | tf_op jit(solution)/shard_map/mto,ti->omi/dot_general | solution.py:241
  333.7 63.7 %collective-permute-done.16 = bf16[384,1280]{1,0:T(8,128)(2,1)S(1)} collective-permute-done((bf16[384,1280]{1,0:T(8,128)(2,1)S(1)}, bf16[384,1280]{1,0:T(8,128)(2,1)S(1)}, u32[]{:S(2)}, u32[]{:S(2)}) %collective-permute-start.16) | collective-permute-done | bytes 983072 | tf_op jit(solution)/shard_map/ppermute | solution.py:38
  399.7 3.8 bitcast_add_fusion
  404.2 13.7 %fusion.77 = f32[6,320,8]{1,2,0:T(8,128)S(1)} fusion(f32[6,1280,8]{1,2,0:T(8,128)S(1)} %copy-done, f32[320,6,1280]{2,0,1:T(8,128)} %param.13, f32[320,3,1280]{2,0,1:T(8,128)S(1)} %bitcast_add_fusion, f32[320,3,1280]{2,0,1:T(8,128)S(1)} %bitcast.236), kind=kOutput, calls=%fused_computation.191 | convolution fusion | flops 240844800 | bytes 19968000 | tf_op jit(solution)/shard_map/omi,mir->rmo/dot_general | solution.py:264
  436.8 9.5 %fusion.38 = bf16[8,6,1280]{2,0,1:T(8,128)(2,1)S(1)} fusion(f32[8,6,320]{2,1,0:T(8,128)} %ortho.1, f32[320,6,1280]{2,0,1:T(8,128)} %param.13, f32[320,3,1280]{2,0,1:T(8,128)} %copy-done.1, f32[320,3,1280]{2,0,1:T(8,128)} %convolution_bitcast_fusion.2), kind=kOutput, calls=%fused_computation.70 | convolution fusion | flops 240906240 | bytes 19845120 | tf_op jit(solution)/shard_map/omi,rmo->rmi/dot_general | solution.py:266
  460.9 4.6 collective-permute-done.24
  465.6 15.7 %bitcast_subtract_fusion = (f32[320,6,1280]{2,0,1:T(8,128)}, f32[6,1280,320]{1,2,0:T(8,128)}) fusion(f32[320,6,1280]{2,0,1:T(8,128)S(1)} %bitcast.234, f32[320,3,1280]{2,0,1:T(8,128)} %copy-done.1, f32[320,3,1280]{2,0,1:T(8,128)} %convolution_bitcast_fusion.2, f32[8,6,320]{2,1,0:T(8,128)S(1)} %copy-done.32, ...), kind=kOutput, calls=%fused_computation.9 | convolution fusion | flops 243548160 | bytes 39628800 | tf_op jit(solution)/shard_map/rmo,rmi->omi/dot_general | solution.py:269
  481.2 5.0 %broadcast_multiply_fusion = (f32[320,6,160]{2,0,1:T(8,128)S(1)}, f32[320,6,160]{2,0,1:T(8,128)}, f32[320,6,160]{2,0,1:T(8,128)}) fusion(f32[320,6,160]{2,0,1:T(8,128)} %copy.78, f32[6,1280,320]{1,2,0:T(8,128)} %get-tuple-element.86, s32[]{:T(128)S(6)} %select_n.243), kind=kLoop, calls=%fused_computation.102 | loop fusion | flops 921600 | bytes 6144004 | tf_op jit(solution)/shard_map/mul | solution.py:276
  (258 shorter events, 139.8 us)
Async XLA Ops:
  0.6 402.9 %copy-start = (f32[6,1280,8]{1,2,0:T(8,128)S(1)}, f32[6,1280,8]{1,2,0:T(8,128)}, u32[]{:S(2)}) copy-start(f32[6,1280,8]{1,2,0:T(8,128)} %param.14) | copy-start | bytes 737284
  0.7 26.6 %collective-permute-start.3 = (bf16[5,320]{1,0:T(8,128)(2,1)}, bf16[5,320]{1,0:T(8,128)(2,1)S(1)}, u32[]{:S(2)}, u32[]{:S(2)}) collective-permute-start(bf16[5,320]{1,0:T(8,128)(2,1)} %param.12), channel_id=1, source_target_pairs={{0,1},{1,0},{2,3},{3,2},{4,5},{5,4},{6,7},{7,6},{8,9},{9,8},{10,11... | collective-permute-start | bytes 9608 | tf_op jit(solution)/shard_map/ppermute | solution.py:34
  1.2 27.8 %collective-permute-start.4 = (bf16[5,320]{1,0:T(8,128)(2,1)}, bf16[5,320]{1,0:T(8,128)(2,1)S(1)}, u32[]{:S(2)}, u32[]{:S(2)}) collective-permute-start(bf16[5,320]{1,0:T(8,128)(2,1)} %param.12), channel_id=1, source_target_pairs={{0,2},{1,3},{2,0},{3,1},{4,6},{5,7},{6,4},{7,5},{8,10},{9,11},{10,... | collective-permute-start | bytes 9608 | tf_op jit(solution)/shard_map/ppermute | solution.py:38
  3.8 27.0 %collective-permute-start = (bf16[384,1280]{1,0:T(8,128)(2,1)}, bf16[384,1280]{1,0:T(8,128)(2,1)S(1)}, u32[]{:S(2)}, u32[]{:S(2)}) collective-permute-start(bf16[384,1280]{1,0:T(8,128)(2,1)} %param.9), channel_id=1, source_target_pairs={{0,1},{1,0},{2,3},{3,2},{4,5},{5,4},{6,7},{7,6},{8,9},{9,8},{10,11... | collective-permute-start | bytes 2949128 | tf_op jit(solution)/shard_map/ppermute | solution.py:34
  3.9 26.7 %collective-permute-start.1 = (bf16[384,1280]{1,0:T(8,128)(2,1)}, bf16[384,1280]{1,0:T(8,128)(2,1)}, u32[]{:S(2)}, u32[]{:S(2)}) collective-permute-start(bf16[384,1280]{1,0:T(8,128)(2,1)} %param.9), channel_id=1, source_target_pairs={{0,2},{1,3},{2,0},{3,1},{4,6},{5,7},{6,4},{7,5},{8,10},{9,11},{10,... | collective-permute-start | bytes 2949128 | tf_op jit(solution)/shard_map/ppermute | solution.py:38
  7.5 103.8 %collective-permute-start.9 = (bf16[320,3,1280]{2,0,1:T(8,128)(2,1)}, bf16[320,3,1280]{2,0,1:T(8,128)(2,1)}, u32[]{:S(2)}, u32[]{:S(2)}) collective-permute-start(bf16[320,3,1280]{2,0,1:T(8,128)(2,1)} %slice.55), channel_id=1, source_target_pairs={{0,1},{1,0},{2,3},{3,2},{4,5},{5,4},{6,7},{7,6},{8,9},{9,8},{10,11... | collective-permute-start | bytes 7372808 | tf_op jit(solution)/shard_map/ppermute | solution.py:34
  27.3 56.0 %collective-permute-start.10 = (bf16[320,3,1280]{2,0,1:T(8,128)(2,1)}, bf16[320,3,1280]{2,0,1:T(8,128)(2,1)}, u32[]{:S(2)}, u32[]{:S(2)}) collective-permute-start(bf16[320,3,1280]{2,0,1:T(8,128)(2,1)} %slice.55), channel_id=1, source_target_pairs={{0,2},{1,3},{2,0},{3,1},{4,6},{5,7},{6,4},{7,5},{8,10},{9,11},{10,... | collective-permute-start | bytes 7372808 | tf_op jit(solution)/shard_map/ppermute | solution.py:38
  29.1 1.2 collective-permute-start.5
  30.7 3.4 collective-permute-start.2
  83.3 44.2 %collective-permute-start.11 = (bf16[320,3,1280]{2,0,1:T(8,128)(2,1)}, bf16[320,3,1280]{2,0,1:T(8,128)(2,1)}, u32[]{:S(2)}, u32[]{:S(2)}) collective-permute-start(bf16[320,3,1280]{2,0,1:T(8,128)(2,1)} %collective-permute-done.10), channel_id=1, source_target_pairs={{0,1},{1,0},{2,3},{3,2},{4,5},{5,4},{6,7},{7,6},{8,9},{9,8},{10,11... | collective-permute-start | bytes 7372808 | tf_op jit(solution)/shard_map/ppermute | solution.py:34
  104.9 5.7 %collective-permute-start.6 = (bf16[384,320]{0,1:T(8,128)(2,1)S(1)}, bf16[384,320]{0,1:T(8,128)(2,1)S(1)}, u32[]{:S(2)}, u32[]{:S(2)}) collective-permute-start(bf16[384,320]{0,1:T(8,128)(2,1)S(1)} %bitcast.257), channel_id=1, source_target_pairs={{0,1},{1,0},{2,3},{3,2},{4,5},{5,4},{6,7},{7,6},{8,9},{9,8},{10,11... | collective-permute-start | bytes 737288 | tf_op jit(solution)/shard_map/ppermute | solution.py:34
  106.9 13.3 %collective-permute-start.7 = (bf16[2,384,320]{1,2,0:T(8,128)(2,1)S(1)}, bf16[2,384,320]{1,2,0:T(8,128)(2,1)S(1)}, u32[]{:S(2)}, u32[]{:S(2)}) collective-permute-start(bf16[2,384,320]{1,2,0:T(8,128)(2,1)S(1)} %bitcast.256), channel_id=1, source_target_pairs={{0,2},{1,3},{2,0},{3,1},{4,6},{5,7},{6,4},{7,5},{8,10},{9,11},{10,... | collective-permute-start | bytes 1474568 | tf_op jit(solution)/shard_map/ppermute | solution.py:38
  120.9 3.3 collective-permute-start.8
  169.2 16.4 %collective-permute-start.13 = (bf16[2,384,320]{1,2,0:T(8,128)(2,1)}, bf16[2,384,320]{1,2,0:T(8,128)(2,1)}, u32[]{:S(2)}, u32[]{:S(2)}) collective-permute-start(bf16[2,384,320]{1,2,0:T(8,128)(2,1)} %dynamic-slice_bitcast_fusion.2), channel_id=1, source_target_pairs={{0,2},{1,3},{2,0},{3,1},{4,6},{5,7},{6,4},{7,5},{8,10},{9,11},{10,... | collective-permute-start | bytes 1474568 | tf_op jit(solution)/shard_map/ppermute | solution.py:38
  171.0 13.9 %collective-permute-start.12 = (bf16[384,320]{0,1:T(8,128)(2,1)}, bf16[384,320]{0,1:T(8,128)(2,1)S(1)}, u32[]{:S(2)}, u32[]{:S(2)}) collective-permute-start(bf16[384,320]{0,1:T(8,128)(2,1)} %dynamic-slice_bitcast_fusion.4), channel_id=1, source_target_pairs={{0,1},{1,0},{2,3},{3,2},{4,5},{5,4},{6,7},{7,6},{8,9},{9,8},{10,11... | collective-permute-start | bytes 737288 | tf_op jit(solution)/shard_map/ppermute | solution.py:34
  187.5 14.0 %collective-permute-start.14 = (bf16[384,320]{0,1:T(8,128)(2,1)}, bf16[384,320]{0,1:T(8,128)(2,1)S(1)}, u32[]{:S(2)}, u32[]{:S(2)}) collective-permute-start(bf16[384,320]{0,1:T(8,128)(2,1)} %get-tuple-element.64), channel_id=1, source_target_pairs={{0,1},{1,0},{2,3},{3,2},{4,5},{5,4},{6,7},{7,6},{8,9},{9,8},{10,11... | collective-permute-start | bytes 737288 | tf_op jit(solution)/shard_map/ppermute | solution.py:34
  201.0 112.8 %collective-permute-start.17 = (bf16[2,320,3,1280]{3,1,2,0:T(8,128)(2,1)}, bf16[2,320,3,1280]{3,1,2,0:T(8,128)(2,1)}, u32[]{:S(2)}, u32[]{:S(2)}) collective-permute-start(bf16[2,320,3,1280]{3,1,2,0:T(8,128)(2,1)} %bitcast.225), channel_id=1, source_target_pairs={{0,1},{1,0},{2,3},{3,2},{4,5},{5,4},{6,7},{7,6},{8,9},{9,8},{10,11... | collective-permute-start | bytes 14745608 | tf_op jit(solution)/shard_map/ppermute | solution.py:34
  312.6 8.3 %collective-permute-start.15 = (bf16[2,384,1280]{2,1,0:T(8,128)(2,1)S(1)}, bf16[2,384,1280]{2,1,0:T(8,128)(2,1)}, u32[]{:S(2)}, u32[]{:S(2)}) collective-permute-start(bf16[2,384,1280]{2,1,0:T(8,128)(2,1)S(1)} %dynamic-slice_bitcast_fusion.1), channel_id=1, source_target_pairs={{0,1},{1,0},{2,3},{3,2},{4,5},{5,4},{6,7},{7,6},{8,9},{9,8},{10,11... | collective-permute-start | bytes 5898248 | tf_op jit(solution)/shard_map/ppermute | solution.py:34
  320.5 79.2 %collective-permute-start.18 = (bf16[320,3,1280]{2,0,1:T(8,128)(2,1)}, bf16[320,3,1280]{2,0,1:T(8,128)(2,1)}, u32[]{:S(2)}, u32[]{:S(2)}) collective-permute-start(bf16[320,3,1280]{2,0,1:T(8,128)(2,1)} %fusion.37), channel_id=1, source_target_pairs={{0,2},{1,3},{2,0},{3,1},{4,6},{5,7},{6,4},{7,5},{8,10},{9,11},{10,... | collective-permute-start | bytes 7372808 | tf_op jit(solution)/shard_map/ppermute | solution.py:38
  327.4 70.0 %copy-start.3 = (f32[2,384,1280]{2,1,0:T(8,128)}, f32[2,384,1280]{2,1,0:T(8,128)S(1)}, u32[]{:S(2)}) copy-start(f32[2,384,1280]{2,1,0:T(8,128)S(1)} %convert_add_fusion.1) | copy-start | bytes 11796484
  327.5 69.8 %collective-permute-start.16 = (bf16[384,1280]{1,0:T(8,128)(2,1)S(1)}, bf16[384,1280]{1,0:T(8,128)(2,1)S(1)}, u32[]{:S(2)}, u32[]{:S(2)}) collective-permute-start(bf16[384,1280]{1,0:T(8,128)(2,1)S(1)} %fusion.50), channel_id=1, source_target_pairs={{0,2},{1,3},{2,0},{3,1},{4,6},{5,7},{6,4},{7,5},{8,10},{9,11},{10,... | collective-permute-start | bytes 2949128 | tf_op jit(solution)/shard_map/ppermute | solution.py:38
  398.4 1.2 collective-permute-start.25
  417.9 4.9 collective-permute-start.19
  419.5 5.0 %collective-permute-start.26 = (f32[4,320]{1,0:T(4,128)S(1)}, f32[4,320]{1,0:T(4,128)S(1)}, u32[]{:S(2)}, u32[]{:S(2)}) collective-permute-start(f32[4,320]{1,0:T(4,128)S(1)} %fusion.64), channel_id=1, source_target_pairs={{0,2},{1,3},{2,0},{3,1},{4,6},{5,7},{6,4},{7,5},{8,10},{9,11},{10,... | collective-permute-start | bytes 15368 | tf_op jit(solution)/shard_map/ppermute | solution.py:38
  422.9 4.7 collective-permute-start.20
  427.6 5.6 %collective-permute-start.21 = (f32[8,6,320]{2,1,0:T(8,128)S(1)}, f32[8,6,320]{2,1,0:T(8,128)S(1)}, u32[]{:S(2)}, u32[]{:S(2)}) collective-permute-start(f32[8,6,320]{2,1,0:T(8,128)S(1)} %add.431), channel_id=1, source_target_pairs={{0,16},{4,20},{8,24},{12,28},{16,0},{20,4},{24,8},{28,12},{1,17},{... | collective-permute-start | bytes 184328 | tf_op jit(solution)/shard_map/ppermute | solution.py:92
  430.2 17.6 %collective-permute-start.27 = (f32[5,320]{1,0:T(8,128)S(1)}, f32[5,320]{1,0:T(8,128)S(1)}, u32[]{:S(2)}, u32[]{:S(2)}) collective-permute-start(f32[5,320]{1,0:T(8,128)S(1)} %pad_maximum_fusion.4), channel_id=1, source_target_pairs={{0,4},{4,0},{8,12},{12,8},{16,20},{20,16},{24,28},{28,24},{1,5},{5... | collective-permute-start | bytes 19208 | tf_op jit(solution)/shard_map/ppermute | solution.py:92
  446.3 4.9 collective-permute-start.22
  447.9 7.1 %collective-permute-start.28 = (f32[5,320]{1,0:T(8,128)S(1)}, f32[5,320]{1,0:T(8,128)S(1)}, u32[]{:S(2)}, u32[]{:S(2)}) collective-permute-start(f32[5,320]{1,0:T(8,128)S(1)} %fusion.70), channel_id=1, source_target_pairs={{0,8},{4,12},{8,0},{12,4},{16,24},{20,28},{24,16},{28,20},{1,9},{5... | collective-permute-start | bytes 19208 | tf_op jit(solution)/shard_map/ppermute | solution.py:92
  451.3 7.1 %collective-permute-start.23 = (bf16[8,6,1280]{2,0,1:T(8,128)(2,1)S(1)}, bf16[8,6,1280]{2,0,1:T(8,128)(2,1)S(1)}, u32[]{:S(2)}, u32[]{:S(2)}) collective-permute-start(bf16[8,6,1280]{2,0,1:T(8,128)(2,1)S(1)} %add_convert_fusion.1), channel_id=1, source_target_pairs={{0,8},{4,12},{8,0},{12,4},{16,24},{20,28},{24,16},{28,20},{1,9},{5... | collective-permute-start | bytes 368648 | tf_op jit(solution)/shard_map/ppermute | solution.py:92
  455.0 5.3 %collective-permute-start.29 = (f32[5,320]{1,0:T(8,128)S(1)}, f32[5,320]{1,0:T(8,128)S(1)}, u32[]{:S(2)}, u32[]{:S(2)}) collective-permute-start(f32[5,320]{1,0:T(8,128)S(1)} %add.441), channel_id=1, source_target_pairs={{0,16},{4,20},{8,24},{12,28},{16,0},{20,4},{24,8},{28,12},{1,17},{... | collective-permute-start | bytes 19208 | tf_op jit(solution)/shard_map/ppermute | solution.py:92
  458.4 7.2 %collective-permute-start.24 = (bf16[8,6,1280]{2,0,1:T(8,128)(2,1)S(1)}, bf16[8,6,1280]{2,0,1:T(8,128)(2,1)S(1)}, u32[]{:S(2)}, u32[]{:S(2)}) collective-permute-start(bf16[8,6,1280]{2,0,1:T(8,128)(2,1)S(1)} %add_convert_fusion), channel_id=1, source_target_pairs={{0,16},{4,20},{8,24},{12,28},{16,0},{20,4},{24,8},{28,12},{1,17},{... | collective-permute-start | bytes 368648 | tf_op jit(solution)/shard_map/ppermute | solution.py:92
  (49 other events, 678.0 us)
